TPU v7x, 32 devices: a whole 2x2x4 slice. The times are simulated.
32 devices in a mesh: group: 4 (over x, core), replica: 8 (over z, y).
Axes of the slice: x: 2, y: 2, z: 4, core: 2. Of those that a mesh axis runs over, the one named last changes fastest.
Arguments:
- activations: float32 [16, 1024, 768], P('replica', 'group'), may hold values from -6 to 6
- out_grad: float32 [16, 1024, 768], P('replica', 'group'), may hold values from -6 to 6
- picture_ids: int32 [16, 1024], P('replica'), may hold values from -1 to 9, as said below
- ln1_gain: float32 [768], P('group'), may hold values from 0.5 to 1.5
- ln1_bias: float32 [768], P('group'), may hold values from -3 to 3
- w_query: float32 [768, 768], P(None, 'group'), may hold values from -0.3125 to 0.3125
- q_bias: float32 [768], P('group'), may hold values from -3 to 3
- w_key: float32 [768, 768], P(None, 'group'), may hold values from -0.3125 to 0.3125
- w_value: float32 [768, 768], P(None, 'group'), may hold values from -0.21875 to 0.21875
- v_bias: float32 [768], P('group'), may hold values from -3 to 3
- w_out: float32 [768, 768], P('group'), may hold values from -1.75 to 1.75
- out_bias: float32 [768], P('group'), may hold values from -3 to 3
- ln2_gain: float32 [768], P('group'), may hold values from 0.5 to 1.5
- ln2_bias: float32 [768], P('group'), may hold values from -3 to 3
- w_fc1: float32 [768, 3072], P(None, 'group'), may hold values from -0.21875 to 0.21875
- fc1_bias: float32 [3072], P('group'), may hold values from -3 to 3
- w_fc2: float32 [3072, 768], P('group'), may hold values from -0.109375 to 0.109375
- fc2_bias: float32 [768], P('group'), may hold values from -3 to 3
Outputs:
- output: float32 [16, 1024, 768], P('replica', 'group')
- grad_input: float32 [16, 1024, 768], P('replica', 'group')
- grad_ln1_gain: float32 [768], P('group')
- grad_ln1_bias: float32 [768], P('group')
- grad_w_query: float32 [768, 768], P(None, 'group')
- grad_q_bias: float32 [768], P('group')
- grad_w_key: float32 [768, 768], P(None, 'group')
- grad_w_value: float32 [768, 768], P(None, 'group')
- grad_v_bias: float32 [768], P('group')
- grad_w_out: float32 [768, 768], P('group')
- grad_out_bias: float32 [768], P('group')
- grad_ln2_gain: float32 [768], P('group')
- grad_ln2_bias: float32 [768], P('group')
- grad_w_fc1: float32 [768, 3072], P(None, 'group')
- grad_fc1_bias: float32 [3072], P('group')
- grad_w_fc2: float32 [3072, 768], P('group')
- grad_fc2_bias: float32 [768], P('group')
Inputs may be any that keep to these rules, and one draw needn't show every extreme that they name: `picture_ids`: each row holds whole pictures numbered 0, 1, 2 and so on from its start, each of 100 to 1024 patches, followed by padding marked -1.
All inputs are finite; a program needn't handle non-finite values.
Results may differ from a plain program's by a relative error of at most 0.04.
Values may be sent and summed in bfloat16 or wider, within the bound.
No kernel may reach another device: no remote copies, remote signals or barrier semaphores. Data moves between devices by JAX's collectives and lax.ppermute only.
A program may use at most 256 MiB of HBM per device.

v0:
```python
import jax
import jax.numpy as jnp
from jax import lax
from jax.sharding import PartitionSpec as P

HEADS = 12
HEAD_DIM = 64
EPS = 1e-06
MASKED = -1e30


def to_float(values):
    return values.astype(jnp.float32)


def normalize(values):
    centred = values - jnp.mean(values, axis=-1, keepdims=True)
    inverse = lax.rsqrt(jnp.mean(centred * centred, axis=-1, keepdims=True) + EPS)
    return (centred * inverse, inverse)


def norm_back(grad_hat, normed_hat, inverse):
    return inverse * (
        grad_hat
        - jnp.mean(grad_hat, axis=-1, keepdims=True)
        - normed_hat * jnp.mean(grad_hat * normed_hat, axis=-1, keepdims=True)
    )


def gelu_tanh(values):
    return jax.nn.gelu(values, approximate=True)


def heads_of(values):
    return values.reshape(values.shape[0], HEADS, HEAD_DIM)


def scores_of(query_rows, key_rows, query_ids, key_ids):
    raw_scores = jnp.einsum(
        "qhe,khe->hqk", heads_of(query_rows), heads_of(key_rows), preferred_element_type=jnp.float32
    ) * HEAD_DIM ** (-0.5)
    allowed = query_ids[:, None] == key_ids[None, :]
    return jnp.where(allowed[None], raw_scores, MASKED)


def attend_row(pieces):
    query_rows, key_rows, value_rows, query_ids, key_ids = pieces
    scores = scores_of(query_rows, key_rows, query_ids, key_ids)
    row_top = jnp.max(scores, axis=-1, keepdims=True)
    exponent = jnp.exp(scores - row_top)
    row_total = jnp.sum(exponent, axis=-1, keepdims=True)
    probability = (exponent / row_total).astype(jnp.bfloat16)
    attended = jnp.einsum(
        "hqk,khe->qhe", probability, heads_of(value_rows), preferred_element_type=jnp.float32
    )
    return (
        attended.reshape(query_rows.shape[0], -1).astype(jnp.bfloat16),
        (row_top + jnp.log(row_total))[..., 0],
    )


def attend_back(pieces):
    query_rows, key_rows, value_rows, query_ids, key_ids, logsum, grad_rows = pieces
    scores = scores_of(query_rows, key_rows, query_ids, key_ids)
    probability = jnp.exp(scores - logsum[..., None])
    grad_heads = heads_of(grad_rows)
    grad_value = jnp.einsum(
        "hqk,qhe->khe",
        probability.astype(jnp.bfloat16),
        grad_heads,
        preferred_element_type=jnp.float32,
    )
    grad_probs = jnp.einsum(
        "qhe,khe->hqk", grad_heads, heads_of(value_rows), preferred_element_type=jnp.float32
    )
    centre = jnp.sum(probability * grad_probs, axis=-1, keepdims=True)
    grad_scores = (probability * (grad_probs - centre)).astype(jnp.bfloat16)
    score_scale = HEAD_DIM ** (-0.5)
    grad_query = (
        jnp.einsum(
            "hqk,khe->qhe", grad_scores, heads_of(key_rows), preferred_element_type=jnp.float32
        )
        * score_scale
    )
    grad_key = (
        jnp.einsum(
            "hqk,qhe->khe", grad_scores, heads_of(query_rows), preferred_element_type=jnp.float32
        )
        * score_scale
    )
    query_count = query_rows.shape[0]
    key_count = key_rows.shape[0]
    return (
        grad_query.reshape(query_count, -1).astype(jnp.bfloat16),
        grad_key.reshape(key_count, -1),
        grad_value.reshape(key_count, -1),
    )


def per_device(
    activations,
    out_grad,
    picture_ids,
    ln1_gain,
    ln1_bias,
    w_query,
    q_bias,
    w_key,
    w_value,
    v_bias,
    w_out,
    out_bias,
    ln2_gain,
    ln2_bias,
    w_fc1,
    fc1_bias,
    w_fc2,
    fc2_bias,
):
    row_block, local_len, width = activations.shape
    row_total = row_block * local_len
    offset = lax.axis_index("group") * local_len
    own_ids = lax.dynamic_slice_in_dim(picture_ids, offset, local_len, 1)
    (
        query_full,
        key_full,
        value_full,
        out_full,
        gain_one,
        shift_one,
        bias_query,
        bias_value,
        bias_out,
        gain_two,
        shift_two,
        bias_fc2,
    ) = (
        lax.all_gather(w_query.astype(jnp.bfloat16), "group", axis=1, tiled=True),
        lax.all_gather(w_key.astype(jnp.bfloat16), "group", axis=1, tiled=True),
        lax.all_gather(w_value.astype(jnp.bfloat16), "group", axis=1, tiled=True),
        lax.all_gather(w_out.astype(jnp.bfloat16), "group", axis=0, tiled=True),
        lax.all_gather(ln1_gain.astype(jnp.bfloat16), "group", axis=0, tiled=True),
        lax.all_gather(ln1_bias.astype(jnp.bfloat16), "group", axis=0, tiled=True),
        lax.all_gather(q_bias.astype(jnp.bfloat16), "group", axis=0, tiled=True),
        lax.all_gather(v_bias.astype(jnp.bfloat16), "group", axis=0, tiled=True),
        lax.all_gather(out_bias.astype(jnp.bfloat16), "group", axis=0, tiled=True),
        lax.all_gather(ln2_gain.astype(jnp.bfloat16), "group", axis=0, tiled=True),
        lax.all_gather(ln2_bias.astype(jnp.bfloat16), "group", axis=0, tiled=True),
        lax.all_gather(fc2_bias.astype(jnp.bfloat16), "group", axis=0, tiled=True),
    )
    inputs = activations.reshape(row_total, width)
    hat_one, inverse_one = normalize(inputs)
    normed_one = (hat_one * to_float(gain_one) + to_float(shift_one)).astype(jnp.bfloat16)
    queries = (
        jnp.dot(normed_one, query_full, preferred_element_type=jnp.float32) + to_float(bias_query)
    ).astype(jnp.bfloat16)
    keys_new = jnp.dot(normed_one, key_full, preferred_element_type=jnp.float32).astype(
        jnp.bfloat16
    )
    values_new = (
        jnp.dot(normed_one, value_full, preferred_element_type=jnp.float32) + to_float(bias_value)
    ).astype(jnp.bfloat16)
    key_all, value_all = (
        lax.all_gather(keys_new.reshape(row_block, local_len, width), "group", axis=1, tiled=True),
        lax.all_gather(
            values_new.reshape(row_block, local_len, width), "group", axis=1, tiled=True
        ),
    )
    query_rows = queries.reshape(row_block, local_len, width)
    attended, logsum = lax.map(attend_row, (query_rows, key_all, value_all, own_ids, picture_ids))
    attended = attended.reshape(row_total, width)
    middle = inputs + (
        jnp.dot(attended, out_full, preferred_element_type=jnp.float32) + to_float(bias_out)
    )
    hat_two, inverse_two = normalize(middle)
    normed_two = (hat_two * to_float(gain_two) + to_float(shift_two)).astype(jnp.bfloat16)
    fc1_full, fc2_full, bias_fc1 = (
        lax.all_gather(w_fc1.astype(jnp.bfloat16), "group", axis=1, tiled=True),
        lax.all_gather(w_fc2.astype(jnp.bfloat16), "group", axis=0, tiled=True),
        lax.all_gather(fc1_bias.astype(jnp.bfloat16), "group", axis=0, tiled=True),
    )
    hidden = jnp.dot(normed_two, fc1_full, preferred_element_type=jnp.float32) + to_float(bias_fc1)
    gelu_value, gelu_pull = jax.vjp(gelu_tanh, hidden)
    activated = gelu_value.astype(jnp.bfloat16)
    mlp_output = jnp.dot(activated, fc2_full, preferred_element_type=jnp.float32)
    output = middle + (mlp_output + to_float(bias_fc2))
    valid_rows = (own_ids >= 0).astype(jnp.float32).reshape(row_total, 1)
    grad_out = out_grad.reshape(row_total, width) * valid_rows
    grad_mlp = grad_out.astype(jnp.bfloat16)
    grad_bias_fc2 = jnp.sum(to_float(grad_mlp), axis=0)
    grad_activated = jnp.dot(grad_mlp, fc2_full.T, preferred_element_type=jnp.float32)
    grad_fc2 = jnp.dot(activated.T, grad_mlp, preferred_element_type=jnp.float32)
    grad_hidden = gelu_pull(grad_activated)[0].astype(jnp.bfloat16)
    grad_fc1 = jnp.dot(normed_two.T, grad_hidden, preferred_element_type=jnp.float32)
    grad_bias_fc1 = jnp.sum(to_float(grad_hidden), axis=0)
    grad_normed_two = jnp.dot(grad_hidden, fc1_full.T, preferred_element_type=jnp.float32)
    grad_fc1, grad_fc2, grad_bias_fc1 = (
        lax.psum_scatter(
            grad_fc1.astype(jnp.bfloat16), "group", scatter_dimension=1, tiled=True
        ).astype(jnp.float32),
        lax.psum_scatter(
            grad_fc2.astype(jnp.bfloat16), "group", scatter_dimension=0, tiled=True
        ).astype(jnp.float32),
        lax.psum_scatter(
            grad_bias_fc1.astype(jnp.bfloat16), "group", scatter_dimension=0, tiled=True
        ).astype(jnp.float32),
    )
    grad_gain_two = jnp.sum(grad_normed_two * hat_two, axis=0)
    grad_shift_two = jnp.sum(grad_normed_two, axis=0)
    grad_middle = grad_out + norm_back(grad_normed_two * to_float(gain_two), hat_two, inverse_two)
    grad_branch = grad_middle.astype(jnp.bfloat16)
    grad_bias_out = jnp.sum(to_float(grad_branch), axis=0)
    grad_out_full = jnp.dot(attended.T, grad_branch, preferred_element_type=jnp.float32)
    grad_attended = jnp.dot(grad_branch, out_full.T, preferred_element_type=jnp.float32).astype(
        jnp.bfloat16
    )
    grad_att_rows = grad_attended.reshape(row_block, local_len, width)
    grad_queries, key_parts, value_parts = lax.map(
        attend_back, (query_rows, key_all, value_all, own_ids, picture_ids, logsum, grad_att_rows)
    )
    grad_keys, grad_values = (
        lax.psum_scatter(
            key_parts.astype(jnp.bfloat16), "group", scatter_dimension=1, tiled=True
        ).astype(jnp.float32),
        lax.psum_scatter(
            value_parts.astype(jnp.bfloat16), "group", scatter_dimension=1, tiled=True
        ).astype(jnp.float32),
    )
    grad_queries = grad_queries.reshape(row_total, width)
    grad_keys = grad_keys.reshape(row_total, width).astype(jnp.bfloat16)
    grad_values = grad_values.reshape(row_total, width).astype(jnp.bfloat16)
    grad_query_full = jnp.dot(normed_one.T, grad_queries, preferred_element_type=jnp.float32)
    grad_key_full = jnp.dot(normed_one.T, grad_keys, preferred_element_type=jnp.float32)
    grad_value_full = jnp.dot(normed_one.T, grad_values, preferred_element_type=jnp.float32)
    grad_bias_query = jnp.sum(to_float(grad_queries), axis=0)
    grad_bias_value = jnp.sum(to_float(grad_values), axis=0)
    grad_normed_one = jnp.dot(grad_queries, query_full.T, preferred_element_type=jnp.float32)
    grad_normed_one = grad_normed_one + jnp.dot(
        grad_keys, key_full.T, preferred_element_type=jnp.float32
    )
    grad_normed_one = grad_normed_one + jnp.dot(
        grad_values, value_full.T, preferred_element_type=jnp.float32
    )
    grad_gain_one = jnp.sum(grad_normed_one * hat_one, axis=0)
    grad_shift_one = jnp.sum(grad_normed_one, axis=0)
    grad_input = grad_middle + norm_back(grad_normed_one * to_float(gain_one), hat_one, inverse_one)
    (
        grad_query_full,
        grad_key_full,
        grad_value_full,
        grad_out_full,
        grad_gain_one,
        grad_shift_one,
        grad_bias_query,
        grad_bias_value,
        grad_bias_out,
        grad_gain_two,
        grad_shift_two,
        grad_bias_fc2,
    ) = (
        lax.psum_scatter(
            grad_query_full.astype(jnp.bfloat16), "group", scatter_dimension=1, tiled=True
        ).astype(jnp.float32),
        lax.psum_scatter(
            grad_key_full.astype(jnp.bfloat16), "group", scatter_dimension=1, tiled=True
        ).astype(jnp.float32),
        lax.psum_scatter(
            grad_value_full.astype(jnp.bfloat16), "group", scatter_dimension=1, tiled=True
        ).astype(jnp.float32),
        lax.psum_scatter(
            grad_out_full.astype(jnp.bfloat16), "group", scatter_dimension=0, tiled=True
        ).astype(jnp.float32),
        lax.psum_scatter(
            grad_gain_one.astype(jnp.bfloat16), "group", scatter_dimension=0, tiled=True
        ).astype(jnp.float32),
        lax.psum_scatter(
            grad_shift_one.astype(jnp.bfloat16), "group", scatter_dimension=0, tiled=True
        ).astype(jnp.float32),
        lax.psum_scatter(
            grad_bias_query.astype(jnp.bfloat16), "group", scatter_dimension=0, tiled=True
        ).astype(jnp.float32),
        lax.psum_scatter(
            grad_bias_value.astype(jnp.bfloat16), "group", scatter_dimension=0, tiled=True
        ).astype(jnp.float32),
        lax.psum_scatter(
            grad_bias_out.astype(jnp.bfloat16), "group", scatter_dimension=0, tiled=True
        ).astype(jnp.float32),
        lax.psum_scatter(
            grad_gain_two.astype(jnp.bfloat16), "group", scatter_dimension=0, tiled=True
        ).astype(jnp.float32),
        lax.psum_scatter(
            grad_shift_two.astype(jnp.bfloat16), "group", scatter_dimension=0, tiled=True
        ).astype(jnp.float32),
        lax.psum_scatter(
            grad_bias_fc2.astype(jnp.bfloat16), "group", scatter_dimension=0, tiled=True
        ).astype(jnp.float32),
    )
    (
        grad_query_full,
        grad_key_full,
        grad_value_full,
        grad_out_full,
        grad_gain_one,
        grad_shift_one,
        grad_bias_query,
        grad_bias_value,
        grad_bias_out,
        grad_gain_two,
        grad_shift_two,
        grad_bias_fc2,
        grad_fc1,
        grad_fc2,
        grad_bias_fc1,
    ) = lax.psum(
        (
            grad_query_full,
            grad_key_full,
            grad_value_full,
            grad_out_full,
            grad_gain_one,
            grad_shift_one,
            grad_bias_query,
            grad_bias_value,
            grad_bias_out,
            grad_gain_two,
            grad_shift_two,
            grad_bias_fc2,
            grad_fc1,
            grad_fc2,
            grad_bias_fc1,
        ),
        "replica",
    )
    return (
        output.reshape(row_block, local_len, width),
        grad_input.reshape(row_block, local_len, width),
        grad_gain_one,
        grad_shift_one,
        grad_query_full,
        grad_bias_query,
        grad_key_full,
        grad_value_full,
        grad_bias_value,
        grad_out_full,
        grad_bias_out,
        grad_gain_two,
        grad_shift_two,
        grad_fc1,
        grad_bias_fc1,
        grad_fc2,
        grad_bias_fc2,
    )


def solution(mesh):
    placed = (
        P("replica", "group", None),
        P("replica", "group", None),
        P("replica", None),
        P("group"),
        P("group"),
        P(None, "group"),
        P("group"),
        P(None, "group"),
        P(None, "group"),
        P("group"),
        P("group", None),
        P("group"),
        P("group"),
        P("group"),
        P(None, "group"),
        P("group"),
        P("group", None),
        P("group"),
    )
    return jax.shard_map(
        per_device,
        mesh=mesh,
        in_specs=placed,
        out_specs=(
            P("replica", "group", None),
            P("replica", "group", None),
            P("group"),
            P("group"),
            P(None, "group"),
            P("group"),
            P(None, "group"),
            P(None, "group"),
            P("group"),
            P("group", None),
            P("group"),
            P("group"),
            P("group"),
            P(None, "group"),
            P("group"),
            P("group", None),
            P("group"),
        ),
        check_vma=False,
    )
```

profile of v0, /device:TPU:0, one launch (start us, length us, event | category | flops | bytes accessed | tf_op | source)
XLA Modules:
  0.0 935.0 jit_solution(2342156140588591705)
XLA Ops:
  7.3 1.9 convert_element_type.265
  13.8 13.2 %all-reduce.19 = (bf16[768]{0:T(1024)(128)(2,1)S(1)}, bf16[768]{0:T(1024)(128)(2,1)S(1)}, bf16[768]{0:T(1024)(128)(2,1)S(1)}, bf16[768]{0:T(1024)(128)(2,1)S(1)}...) all-reduce(bf16[768]{0:T(1024)(128)(2,1)S(1)} %dynamic-update-slice, ...), channel_id=1, replica_groups=mesh['group'=4,'replica'=8] {'group'}, use_global_device_ids=true, to_apply=%add.1 | all-reduce | flops 5376 | bytes 21504
  28.7 1.9 all-gather.10.cloned.1.call-done
  30.6 2.1 add_convert_fusion.3
  33.9 16.3 %all-gather.16.cloned.1.call-done = bf16[768,768]{0,1:T(8,128)(2,1)} async-done(((bf16[768,192]{0,1:T(8,128)(2,1)}), bf16[768,768]{0,1:T(8,128)(2,1)}) %all-gather.16.cloned.1.call-update) | async-done | bytes 1179664 | tf_op jit(solution)/shard_map/all_gather | solution.py:139
  50.2 2.1 convolution_convert_fusion.4
  54.4 2.8 convert_element_type.283
  57.3 3.0 convert_element_type.287
  62.3 5.2 all-gather
  69.9 2.3 add_convert_fusion.2
  72.5 28.4 %all-gather.12.cloned.1.call-done = bf16[2,1024,768]{1,2,0:T(8,128)(2,1)} async-done(((bf16[2,256,768]{1,2,0:T(8,128)(2,1)}), bf16[2,1024,768]{1,2,0:T(8,128)(2,1)}) %all-gather.12.cloned.1.call-update) | async-done | bytes 3145744 | tf_op jit(solution)/shard_map/all_gather | solution.py:165
  100.9 30.4 %all-gather.18.cloned.1.call-done = bf16[2,1024,768]{1,2,0:T(8,128)(2,1)} async-done(((bf16[2,256,768]{1,2,0:T(8,128)(2,1)}), bf16[2,1024,768]{1,2,0:T(8,128)(2,1)}) %all-gather.18.cloned.1.call-update) | async-done | bytes 3145744 | tf_op jit(solution)/shard_map/all_gather | solution.py:164
  131.2 29.5 %while.26 = (s32[]{:T(128)}, bf16[2,256,768]{2,1,0:T(8,128)(2,1)}, f32[2,12,256]{2,1,0:T(8,128)}, bf16[2,1024,768]{1,2,0:T(8,128)(2,1)}, s32[2,256]{1,0:T(2,128)...) while((s32[]{:T(128)}, bf16[2,256,768]{2,1,0:T(8,128)(2,1)}, ...), condition=%wide.region_5.6_spmd, body=%wide.region_2.5_spmd.sunk | while | flops 843510784 | bytes 51499116 | solution.py:170
  132.3 2.2 constant_dynamic-slice_fusion.23
  134.6 2.3 fusion.100
  136.9 3.6 fusion.101
  141.1 3.9 fusion.102
  147.0 2.2 constant_dynamic-slice_fusion.23
  149.2 2.3 fusion.100
  151.5 3.6 fusion.101
  155.8 3.9 fusion.102
  160.7 2.6 fusion.32
  164.8 25.6 %all-gather.22.cloned.1.call-done = bf16[768,3072]{1,0:T(8,128)(2,1)} async-done(((bf16[768,768]{1,0:T(8,128)(2,1)}), bf16[768,3072]{1,0:T(8,128)(2,1)}) %all-gather.22.cloned.1.call-update) | async-done | bytes 4718608 | tf_op jit(solution)/shard_map/all_gather | solution.py:178
  190.4 8.2 fusion.28
  198.6 31.4 %all-gather.24.cloned.1.call-done = bf16[3072,768]{1,0:T(8,128)(2,1)} async-done(((bf16[768,768]{1,0:T(8,128)(2,1)}), bf16[3072,768]{1,0:T(8,128)(2,1)}) %all-gather.24.cloned.1.call-update) | async-done | bytes 4718608 | tf_op jit(solution)/shard_map/all_gather | solution.py:179
  230.0 9.8 %fusion.29 = (bf16[3072]{0:T(1024)(128)(2,1)}, bf16[512,3072]{1,0:T(8,128)(2,1)S(1)}) fusion(f32[512,3072]{1,0:T(8,128)} %fusion.28, f32[3072]{0:T(1024)S(1)} %bitcast.212, bf16[512,768]{1,0:T(8,128)(2,1)S(1)} %copy-done.22, bf16[3072,768]{1,0:T(8,128)(2,1)} %all-gather.24.cloned.1.call-done), kind=kOutput, calls=%fused_computation.108 | convolution fusion | flops 2450519040 | bytes 14960640 | tf_op jit(solution)/shard_map/dot_general | solution.py:191
  239.8 3.5 multiply_reduce_fusion.1
  245.7 109.7 %while.27 = (s32[]{:T(128)}, bf16[2,256,768]{1,2,0:T(8,128)(2,1)}, bf16[2,1024,768]{2,1,0:T(8,128)(2,1)}, bf16[2,1024,768]{2,1,0:T(8,128)(2,1)}, bf16[2,1024,768...) while((s32[]{:T(128)}, bf16[2,256,768]{1,2,0:T(8,128)(2,1)}, ...), condition=%wide.region_12.13_spmd, body=%wide.region_10.12_spmd.sunk | while | flops 2062676992 | bytes 238015056 | solution.py:218
  246.1 2.1 constant_dynamic-slice_fusion.27
  248.3 6.4 fusion.113
  258.3 11.5 %multiply_reduce_fusion.10 = (f32[12,256]{1,0:T(8,128)S(1)}, f32[12,256,1024]{2,1,0:T(8,128)}) fusion(f32[12,256,1024]{2,1,0:T(8,128)} %fusion.113, f32[12,256]{1,0:T(8,128)S(1)} %dynamic-slice_bitcast_fusion.2, pred[256,1024]{1,0:T(8,128)(4,1)S(1)} %broadcast_compare_fusion.5, bf16[256,12,64]{0,2,1:T(8,128)(2,1)S(1)} %bitcast.188, ...), kind=kOutput, calls=%fused_computation.18.clone.1 | convolution fusion | flops 418378752 | bytes 27418624 | tf_op jit(solution)/shard_map/while/body/eval_jaxpr/qhe,khe->hqk/dot_general | solution.py:73
  270.9 6.7 multiply_convert_fusion.6
  281.8 9.0 fusion.115
  290.8 2.7 copy.97
  293.5 3.5 constant_dynamic-update-slice_fusion.9
  297.9 2.0 fusion.114
  300.8 2.1 constant_dynamic-slice_fusion.27
  302.9 6.4 fusion.113
  313.0 11.5 %multiply_reduce_fusion.10 = (f32[12,256]{1,0:T(8,128)S(1)}, f32[12,256,1024]{2,1,0:T(8,128)}) fusion(f32[12,256,1024]{2,1,0:T(8,128)} %fusion.113, f32[12,256]{1,0:T(8,128)S(1)} %dynamic-slice_bitcast_fusion.2, pred[256,1024]{1,0:T(8,128)(4,1)S(1)} %broadcast_compare_fusion.5, bf16[256,12,64]{0,2,1:T(8,128)(2,1)S(1)} %bitcast.188, ...), kind=kOutput, calls=%fused_computation.18.clone.1 | convolution fusion | flops 418378752 | bytes 27418624 | tf_op jit(solution)/shard_map/while/body/eval_jaxpr/qhe,khe->hqk/dot_general | solution.py:73
  325.6 6.7 multiply_convert_fusion.6
  336.5 9.0 fusion.115
  345.5 2.7 copy.97
  348.2 3.4 constant_dynamic-update-slice_fusion.9
  352.6 2.0 fusion.114
  358.3 3.0 bitcast_convert_fusion.2
  361.4 2.9 convolution_convert_fusion.2
  364.4 29.1 %reduce-scatter.9.cloned.1.call-done = bf16[2,256,768]{2,1,0:T(8,128)(2,1)} async-done(((bf16[2,1024,768]{2,1,0:T(8,128)(2,1)}), bf16[2,256,768]{2,1,0:T(8,128)(2,1)}) %reduce-scatter.9.cloned.1.call-update) | async-done | bytes 786448 | tf_op jit(solution)/shard_map/reduce_scatter | solution.py:222
  393.6 3.2 bitcast_convert_fusion.1
  396.9 37.2 %reduce-scatter.11.cloned.1.call-done = bf16[2,256,768]{2,1,0:T(8,128)(2,1)} async-done(((bf16[2,1024,768]{2,1,0:T(8,128)(2,1)}), bf16[2,256,768]{2,1,0:T(8,128)(2,1)}) %reduce-scatter.11.cloned.1.call-update) | async-done | bytes 786448 | tf_op jit(solution)/shard_map/reduce_scatter | solution.py:225
  434.1 3.3 bitcast_convert_fusion
  437.5 7.4 convolution_convert_fusion.1
  445.6 8.9 convolution_convert_fusion
  458.3 2.3 copy.57
  461.9 3.4 fusion.34
  465.4 26.0 %reduce-scatter.19.cloned.1.call-done = bf16[192,768]{1,0:T(8,128)(2,1)} async-done(((bf16[768,768]{1,0:T(8,128)(2,1)}), bf16[192,768]{1,0:T(8,128)(2,1)}) %reduce-scatter.19.cloned.1.call-update) | async-done | bytes 294928 | tf_op jit(solution)/shard_map/reduce_scatter | solution.py:270
  492.7 2.4 fusion.35
  495.3 2.4 multiply_reduce_fusion.2
  497.7 10.3 %all-reduce.18 = (bf16[768]{0:T(1024)(128)(2,1)S(1)}, bf16[768]{0:T(1024)(128)(2,1)S(1)}, bf16[768]{0:T(1024)(128)(2,1)S(1)}, bf16[768]{0:T(1024)(128)(2,1)S(1)}...) all-reduce(bf16[768]{0:T(1024)(128)(2,1)S(1)} %dynamic-update-slice, ...), channel_id=1, replica_groups=mesh['group'=4,'replica'=8] {'group'}, use_global_device_ids=true, to_apply=%add.7 | all-reduce | flops 9984 | bytes 39936
  508.6 3.2 multiply_add_fusion
  511.8 9.3 add_add_fusion.1
  521.1 27.5 %reduce-scatter.17.cloned.1.call-done = bf16[768,192]{0,1:T(8,128)(2,1)} async-done(((bf16[768,768]{0,1:T(8,128)(2,1)}), bf16[768,192]{0,1:T(8,128)(2,1)}) %reduce-scatter.17.cloned.1.call-update) | async-done | bytes 294928 | tf_op jit(solution)/shard_map/reduce_scatter | solution.py:267
  548.6 50.2 %reduce-scatter.21.cloned.1.call-done = bf16[768,768]{1,0:T(8,128)(2,1)} async-done(((bf16[768,3072]{1,0:T(8,128)(2,1)}), bf16[768,768]{1,0:T(8,128)(2,1)}) %reduce-scatter.21.cloned.1.call-update) | async-done | bytes 1179664 | tf_op jit(solution)/shard_map/reduce_scatter | solution.py:198
  598.8 50.5 %reduce-scatter.23.cloned.1.call-done = bf16[768,768]{1,0:T(8,128)(2,1)} async-done(((bf16[3072,768]{1,0:T(8,128)(2,1)}), bf16[768,768]{1,0:T(8,128)(2,1)}) %reduce-scatter.23.cloned.1.call-update) | async-done | bytes 1179664 | tf_op jit(solution)/shard_map/reduce_scatter | solution.py:201
  649.3 279.1 %all-reduce.21 = (f32[192]{0:T(256)}, f32[192]{0:T(256)}, f32[768,192]{0,1:T(8,128)}, f32[192]{0:T(256)}, f32[768,192]{0,1:T(8,128)}, /*index=5*/f32[768,192]{0,...) all-reduce(f32[192]{0:T(256)S(1)} %dynamic-slice_convert_fusion.8, ...), channel_id=1, replica_groups=mesh['group'=4,'replica'=8] {'replica'}, use_global_device_ids=true, to_apply=%region_19.20 | all-reduce | flops 1771776 | bytes 10635264 | tf_op jit(solution)/shard_map/psum | solution.py:314
  (335 shorter events, 53.1 us)
Async XLA Ops:
  7.2 2.9 copy-start.26
  7.2 3.7 copy-start.64
  7.2 3.8 copy-start.65
  7.2 3.8 copy-start.66
  7.2 3.8 copy-start.67
  7.3 3.8 copy-start.68
  7.3 3.8 copy-start.69
  7.3 3.8 copy-start.70
  7.3 23.3 %all-gather.10.cloned.1.call-start = ((), (), s32[]{:S(2)}) async-start(), calls=%async_computation.8 | async-start | bytes 1474560 | tf_op jit(solution)/shard_map/all_gather | solution.py:140
  9.2 17.8 %copy-start.5 = (f32[2,256,768]{2,1,0:T(8,128)S(1)}, f32[2,256,768]{2,1,0:T(8,128)}, u32[]{:S(2)}) copy-start(f32[2,256,768]{2,1,0:T(8,128)} %param.22) | copy-start | bytes 4718596
  9.2 41.0 %all-gather.16.cloned.1.call-start = ((), (), s32[]{:S(2)}) async-start(), calls=%async_computation.11 | async-start | bytes 1474560 | tf_op jit(solution)/shard_map/all_gather | solution.py:139
  10.1 59.8 %all-gather.14.cloned.1.call-start = ((), (), s32[]{:S(2)}) async-start(), calls=%async_computation.10 | async-start | bytes 1474560 | tf_op jit(solution)/shard_map/all_gather | solution.py:138
  10.9 90.0 %all-gather.12.cloned.1.call-start = ((), (), s32[]{:S(2)}) async-start(), calls=%async_computation.9 | async-start | bytes 3932160 | tf_op jit(solution)/shard_map/all_gather | solution.py:165
  28.7 21.5 %copy-start.23 = (bf16[512,768]{1,0:T(8,128)(2,1)}, bf16[512,768]{1,0:T(8,128)(2,1)S(1)}, u32[]{:S(2)}) copy-start(bf16[512,768]{1,0:T(8,128)(2,1)S(1)} %add_convert_fusion.4) | copy-start | bytes 2359300
  33.8 97.4 %all-gather.18.cloned.1.call-start = ((), (), s32[]{:S(2)}) async-start(), calls=%async_computation.12 | async-start | bytes 3932160 | tf_op jit(solution)/shard_map/all_gather | solution.py:164
  53.5 107.2 %all-gather.20.cloned.1.call-start = ((), (), s32[]{:S(2)}) async-start(), calls=%async_computation.13 | async-start | bytes 1474560 | tf_op jit(solution)/shard_map/all_gather | solution.py:141
  54.3 136.0 %all-gather.22.cloned.1.call-start = ((), (), s32[]{:S(2)}) async-start(), calls=%async_computation.14 | async-start | bytes 5898240 | tf_op jit(solution)/shard_map/all_gather | solution.py:178
  57.2 5.1 copy-start.56
  57.2 10.9 %copy-start.12 = (f32[2,256,768]{2,1,0:T(8,128)S(1)}, f32[2,256,768]{2,1,0:T(8,128)}, u32[]{:S(2)}) copy-start(f32[2,256,768]{2,1,0:T(8,128)} %param.23) | copy-start | bytes 4718596
  57.2 172.7 %all-gather.24.cloned.1.call-start = ((), (), s32[]{:S(2)}) async-start(), calls=%async_computation.15 | async-start | bytes 5898240 | tf_op jit(solution)/shard_map/all_gather | solution.py:179
  60.3 333.3 %reduce-scatter.9.cloned.1.call-start = ((), (), s32[]{:S(2)}) async-start(), calls=%async_computation.16 | async-start | bytes 3932160 | tf_op jit(solution)/shard_map/reduce_scatter | solution.py:222
  61.0 182.3 %copy-start.46 = (f32[768]{0:T(1024)}, f32[768]{0:T(1024)S(1)}, u32[]{:S(2)}) copy-start(f32[768]{0:T(1024)S(1)} %convert_element_type.279) | copy-start | bytes 9220
  61.0 129.4 %copy-start.57 = (f32[768]{0:T(1024)}, f32[768]{0:T(1024)S(1)}, u32[]{:S(2)}) copy-start(f32[768]{0:T(1024)S(1)} %convert_element_type.281) | copy-start | bytes 9220
  62.3 6.9 copy-start.44
  163.3 80.0 %copy-start.42 = (f32[512]{0:T(512)}, f32[512]{0:T(512)S(1)}, u32[]{:S(2)}) copy-start(f32[512]{0:T(512)S(1)} %broadcast_multiply_fusion.4) | copy-start | bytes 6148
  164.8 78.5 %copy-start.53 = (f32[512]{0:T(512)}, f32[512]{0:T(512)S(1)}, u32[]{:S(2)}) copy-start(f32[512]{0:T(512)S(1)} %add_rsqrt_fusion) | copy-start | bytes 6148
  164.8 65.2 %copy-start.22 = (bf16[512,768]{1,0:T(8,128)(2,1)S(1)}, bf16[512,768]{1,0:T(8,128)(2,1)}, u32[]{:S(2)}) copy-start(bf16[512,768]{1,0:T(8,128)(2,1)} %fusion.21) | copy-start | bytes 2359300
  164.8 65.2 %copy-start.48 = (f32[4,1,768]{2,1,0:T(1,128)S(1)}, f32[4,1,768]{2,1,0:T(1,128)}, u32[]{:S(2)}) copy-start(f32[4,1,768]{2,1,0:T(1,128)} %convert_element_type.326) | copy-start | bytes 36868
  230.0 9.8 %copy-start.15 = (f32[512,768]{1,0:T(8,128)S(1)}, f32[512,768]{1,0:T(8,128)}, u32[]{:S(2)}) copy-start(f32[512,768]{1,0:T(8,128)} %copy-done.14) | copy-start | bytes 4718596
  230.0 9.8 %copy-start.62 = (bf16[768,3072]{1,0:T(8,128)(2,1)S(1)}, bf16[768,3072]{1,0:T(8,128)(2,1)}, u32[]{:S(2)}) copy-start(bf16[768,3072]{1,0:T(8,128)(2,1)} %all-gather.22.cloned.1.call-done) | copy-start | bytes 14155780
  239.7 3.6 copy-start.72
  239.7 3.6 copy-start.13
  239.7 3.6 copy-start.45
  246.1 9.3 copy-start.32
  246.1 10.3 %copy-start.17 = (bf16[2,256,768]{2,1,0:T(8,128)(2,1)}, bf16[2,256,768]{2,1,0:T(8,128)(2,1)S(1)}, u32[]{:S(2)}) copy-start(bf16[2,256,768]{2,1,0:T(8,128)(2,1)S(1)} %get-tuple-element.477) | copy-start | bytes 2359300 | tf_op jit(solution)/shard_map/while
  255.6 14.3 %copy-start.3 = (pred[256,1024]{1,0:T(8,128)(4,1)}, pred[256,1024]{1,0:T(8,128)(4,1)S(1)}, u32[]{:S(2)}) copy-start(pred[256,1024]{1,0:T(8,128)(4,1)S(1)} %broadcast_compare_fusion.5) | copy-start | bytes 786436 | tf_op jit(solution)/shard_map/while
  258.3 11.6 %slice-start = ((s8[12582912]{0:T(1024)(128)(4,1)}), s8[4194304]{0:T(1024)(128)(4,1)S(1)}, s32[]{:S(2)}) async-start(s8[12582912]{0:T(1024)(128)(4,1)} %bitcast.175), calls=%async_computation.24 | async-start | bytes 8388608 | tf_op jit(solution)/shard_map/while
  258.3 11.6 %slice-start.1 = ((s8[12582912]{0:T(1024)(128)(4,1)}), s8[4194304]{0:T(1024)(128)(4,1)S(1)}, s32[]{:S(2)}) async-start(s8[12582912]{0:T(1024)(128)(4,1)} %bitcast.175), calls=%async_computation.25 | async-start | bytes 8388608 | tf_op jit(solution)/shard_map/while
  258.3 12.6 %slice-start.2 = ((s8[12582912]{0:T(1024)(128)(4,1)}), s8[4194304]{0:T(1024)(128)(4,1)S(1)}, s32[]{:S(2)}) async-start(s8[12582912]{0:T(1024)(128)(4,1)} %bitcast.175), calls=%async_computation.26 | async-start | bytes 8388608 | tf_op jit(solution)/shard_map/while
  293.5 4.4 copy-start.1
  297.9 2.8 copy-start.18
  297.9 2.8 copy-start.33
  300.8 9.3 copy-start.32
  300.8 10.3 %copy-start.17 = (bf16[2,256,768]{2,1,0:T(8,128)(2,1)}, bf16[2,256,768]{2,1,0:T(8,128)(2,1)S(1)}, u32[]{:S(2)}) copy-start(bf16[2,256,768]{2,1,0:T(8,128)(2,1)S(1)} %get-tuple-element.477) | copy-start | bytes 2359300 | tf_op jit(solution)/shard_map/while
  310.3 14.3 %copy-start.3 = (pred[256,1024]{1,0:T(8,128)(4,1)}, pred[256,1024]{1,0:T(8,128)(4,1)S(1)}, u32[]{:S(2)}) copy-start(pred[256,1024]{1,0:T(8,128)(4,1)S(1)} %broadcast_compare_fusion.5) | copy-start | bytes 786436 | tf_op jit(solution)/shard_map/while
  313.0 11.6 %slice-start = ((s8[12582912]{0:T(1024)(128)(4,1)}), s8[4194304]{0:T(1024)(128)(4,1)S(1)}, s32[]{:S(2)}) async-start(s8[12582912]{0:T(1024)(128)(4,1)} %bitcast.175), calls=%async_computation.24 | async-start | bytes 8388608 | tf_op jit(solution)/shard_map/while
  313.0 11.6 %slice-start.1 = ((s8[12582912]{0:T(1024)(128)(4,1)}), s8[4194304]{0:T(1024)(128)(4,1)S(1)}, s32[]{:S(2)}) async-start(s8[12582912]{0:T(1024)(128)(4,1)} %bitcast.175), calls=%async_computation.25 | async-start | bytes 8388608 | tf_op jit(solution)/shard_map/while
  313.0 12.6 %slice-start.2 = ((s8[12582912]{0:T(1024)(128)(4,1)}), s8[4194304]{0:T(1024)(128)(4,1)S(1)}, s32[]{:S(2)}) async-start(s8[12582912]{0:T(1024)(128)(4,1)} %bitcast.175), calls=%async_computation.26 | async-start | bytes 8388608 | tf_op jit(solution)/shard_map/while
  348.2 4.4 copy-start.1
  355.4 78.6 %reduce-scatter.11.cloned.1.call-start = ((), (), s32[]{:S(2)}) async-start(), calls=%async_computation.17 | async-start | bytes 3932160 | tf_op jit(solution)/shard_map/reduce_scatter | solution.py:225
  356.0 109.3 %reduce-scatter.13.cloned.1.call-start = ((), (), s32[]{:S(2)}) async-start(), calls=%async_computation.18 | async-start | bytes 1474560 | tf_op jit(solution)/shard_map/reduce_scatter | solution.py:261
  358.3 3.1 copy-start.11
  361.4 130.0 %reduce-scatter.19.cloned.1.call-start = ((), (), s32[]{:S(2)}) async-start(), calls=%async_computation.21 | async-start | bytes 1474560 | tf_op jit(solution)/shard_map/reduce_scatter | solution.py:270
  364.4 156.7 %reduce-scatter.15.cloned.1.call-start = ((), (), s32[]{:S(2)}) async-start(), calls=%async_computation.19 | async-start | bytes 1474560 | tf_op jit(solution)/shard_map/reduce_scatter | solution.py:264
  396.8 40.6 %copy-start.43 = (f32[512]{0:T(512)S(1)}, f32[512]{0:T(512)}, u32[]{:S(2)}) copy-start(f32[512]{0:T(512)} %copy-done.42) | copy-start | bytes 6148
  396.8 40.6 %copy-start.47 = (f32[768]{0:T(1024)S(1)}, f32[768]{0:T(1024)}, u32[]{:S(2)}) copy-start(f32[768]{0:T(1024)} %copy-done.46) | copy-start | bytes 9220
  396.8 40.6 %copy-start.54 = (f32[512]{0:T(512)S(1)}, f32[512]{0:T(512)}, u32[]{:S(2)}) copy-start(f32[512]{0:T(512)} %copy-done.53) | copy-start | bytes 6148
  396.8 40.6 %copy-start.58 = (f32[768]{0:T(1024)S(1)}, f32[768]{0:T(1024)}, u32[]{:S(2)}) copy-start(f32[768]{0:T(1024)} %copy-done.57) | copy-start | bytes 9220
  396.8 151.8 %reduce-scatter.17.cloned.1.call-start = ((), (), s32[]{:S(2)}) async-start(), calls=%async_computation.20 | async-start | bytes 1474560 | tf_op jit(solution)/shard_map/reduce_scatter | solution.py:267
  437.4 161.5 %reduce-scatter.21.cloned.1.call-start = ((), (), s32[]{:S(2)}) async-start(), calls=%async_computation.22 | async-start | bytes 5898240 | tf_op jit(solution)/shard_map/reduce_scatter | solution.py:198
  444.9 204.4 %reduce-scatter.23.cloned.1.call-start = ((), (), s32[]{:S(2)}) async-start(), calls=%async_computation.23 | async-start | bytes 5898240 | tf_op jit(solution)/shard_map/reduce_scatter | solution.py:201
  508.6 3.2 copy-start.16
  511.8 137.5 %copy-start.28 = (bf16[768,192]{0,1:T(8,128)(2,1)S(1)}, bf16[768,192]{0,1:T(8,128)(2,1)}, u32[]{:S(2)}) copy-start(bf16[768,192]{0,1:T(8,128)(2,1)} %reduce-scatter.13.cloned.1.call-done) | copy-start | bytes 884740
  511.8 137.5 %copy-start.29 = (bf16[192,768]{1,0:T(8,128)(2,1)S(1)}, bf16[192,768]{1,0:T(8,128)(2,1)}, u32[]{:S(2)}) copy-start(bf16[192,768]{1,0:T(8,128)(2,1)} %reduce-scatter.19.cloned.1.call-done) | copy-start | bytes 884740
  (43 other events, 79.7 us)
Sparse Core Ops, SparseCore 0:
  10.3 20.2 all-gather.9
  32.7 17.4 all-gather.15
  52.3 17.5 all-gather.13
  71.9 28.9 all-gather.11
  102.2 28.9 all-gather.17
  133.2 17.4 all-gather.19
  152.8 37.4 all-gather.21
  192.5 37.4 all-gather.23
  355.6 37.9 reduce-scatter.8
  396.1 37.9 reduce-scatter.10
  437.2 25.7 reduce-scatter.12
  465.6 25.7 reduce-scatter.18
  494.5 25.7 reduce-scatter.14
  522.8 25.7 reduce-scatter.16
  551.0 47.8 reduce-scatter.20
  601.4 47.8 reduce-scatter.22
where the time goes:
time: 942 us; the launch traced here: 935 us
  waiting for transfers between devices  356 us (38%)
  blocking collectives  308 us (33%)
  matrix products  151 us (16%)
  local copies, waits for them, and re-layouts  54.9 us (6%)
  other arithmetic  47.5 us (5%)
  between operations  17 us (2%)
    psum x1, blocking collectives, per_device(): lax.psum((grad_query_full, grad_key_full, grad_value_full, grad_out_full,...  279 us
    reduce_scatter x1, waiting for transfers between devices, per_device(): lax.psum_scatter(grad_fc2.astype(jnp.bfloat16), 'group', scatter_dimensio...  50.5 us
    reduce_scatter x1, waiting for transfers between devices, per_device(): lax.psum_scatter(grad_fc1.astype(jnp.bfloat16), 'group', scatter_dimensio...  50.2 us
    reduce_scatter x1, waiting for transfers between devices, per_device(): lax.psum_scatter(value_parts.astype(jnp.bfloat16), 'group', scatter_dimen...  37.2 us
    all_gather x1, waiting for transfers between devices, per_device(): lax.all_gather(w_fc2.astype(jnp.bfloat16), 'group', axis=0, tiled=True)  31.4 us
    all_gather x1, waiting for transfers between devices, per_device(): lax.all_gather(keys_new.reshape(row_block, local_len, width), 'group', ax...  30.4 us
    reduce_scatter x1, waiting for transfers between devices, per_device(): lax.psum_scatter(key_parts.astype(jnp.bfloat16), 'group', scatter_dimensi...  29.1 us
    all_gather x1, waiting for transfers between devices, per_device(): lax.all_gather(values_new.reshape(row_block, local_len, width), 'group',...  28.4 us
  transfers between devices with their start and end apart: 16, of which 13 were waited for; matrix products, arithmetic and copies ran while one was open for 13% of the time, Pallas kernels for 0%

commit v1 on v0

--- a/solution.py
+++ b/solution.py
@@ -1,3 +1,4 @@
+import functools
 import jax
 import jax.numpy as jnp
 from jax import lax
@@ -7,6 +8,22 @@
 HEAD_DIM = 64
 EPS = 1e-06
 MASKED = -1e30
+
+
+def form_regions(frame, axis_key, d0):
+    cores_n = lax.axis_size(axis_key)
+    windows = [frame]
+    for hop_no in range(1, cores_n):
+        view_out = lax.ppermute(
+            windows[hop_no - 1], axis_key, [(k0, (k0 - 1) % cores_n) for k0 in range(cores_n)]
+        )
+        windows.append(view_out)
+    x_next = jnp.concatenate(windows, d0)
+    big = lax.axis_index(axis_key)
+    return jnp.roll(x_next, big * frame.shape[d0], d0)
+
+
+move_vector_here = functools.partial(form_regions, axis_key="group", d0=1)
 
 
 def to_float(values):
@@ -175,7 +192,7 @@
     hat_two, inverse_two = normalize(middle)
     normed_two = (hat_two * to_float(gain_two) + to_float(shift_two)).astype(jnp.bfloat16)
     fc1_full, fc2_full, bias_fc1 = (
-        lax.all_gather(w_fc1.astype(jnp.bfloat16), "group", axis=1, tiled=True),
+        move_vector_here(w_fc1.astype(jnp.bfloat16)),
         lax.all_gather(w_fc2.astype(jnp.bfloat16), "group", axis=0, tiled=True),
         lax.all_gather(fc1_bias.astype(jnp.bfloat16), "group", axis=0, tiled=True),
     )

time: 942 us -> 932 us (0.989)
  waiting for transfers between devices: 356 us -> 291 us
  blocking collectives: 308 us -> 327 us
  local copies, waits for them, and re-layouts: 54.9 us -> 71.5 us
    ppermute x0 -> x3, waiting for transfers between devices: none -> 46.8 us  [form_regions(): lax.ppermute(windows[hop_no - 1], axis_key, [(k0, (k0 - 1) % cores_n) for...]
    all_gather x1, waiting for transfers between devices: 30.4 us -> 0.01 us  [per_device(): lax.all_gather(keys_new.reshape(row_block, local_len, width), 'group', ax...]
    all_gather x1, waiting for transfers between devices: 28.4 us -> 0.01 us  [per_device(): lax.all_gather(values_new.reshape(row_block, local_len, width), 'group',...]
    all_gather x1, waiting for transfers between devices: 31.4 us -> 5.8 us  [per_device(): lax.all_gather(w_fc2.astype(jnp.bfloat16), 'group', axis=0, tiled=True)]
    all_gather x1 -> x0, waiting for transfers between devices: 25.6 us -> none  [per_device(): lax.all_gather(w_fc1.astype(jnp.bfloat16), 'group', axis=1, tiled=True)]
    all_gather x1, blocking collectives: 5.2 us -> 24.1 us  [per_device(): lax.all_gather(fc1_bias.astype(jnp.bfloat16), 'group', axis=0, tiled=True)]
    unnamed x143 -> x149, local copies, waits for them, and re-layouts: 7.43 us -> 22.6 us
  transfers between devices with their start and end apart: 16 -> 18, of which waited for: 13 -> 11; matrix products, arithmetic and copies ran while one was open for 13% -> 15% of each run, Pallas kernels for 0% -> 0%
where the time goes in v1:
time: 932 us; the launch traced here: 924 us
  blocking collectives  327 us (35%)
  waiting for transfers between devices  291 us (31%)
  matrix products  154 us (17%)
  local copies, waits for them, and re-layouts  71.5 us (8%)
  other arithmetic  49.1 us (5%)
  between operations  17.2 us (2%)
  loops' own time  9.64 us (1%)
    psum x1, blocking collectives, per_device(): lax.psum((grad_query_full, grad_key_full, grad_value_full, grad_out_full,...  279 us
    reduce_scatter x1, waiting for transfers between devices, per_device(): lax.psum_scatter(grad_fc1.astype(jnp.bfloat16), 'group', scatter_dimensio...  50.4 us
    reduce_scatter x1, waiting for transfers between devices, per_device(): lax.psum_scatter(grad_fc2.astype(jnp.bfloat16), 'group', scatter_dimensio...  50.3 us
    ppermute x3, waiting for transfers between devices, form_regions(): lax.ppermute(windows[hop_no - 1], axis_key, [(k0, (k0 - 1) % cores_n) for...  46.8 us
    reduce_scatter x1, waiting for transfers between devices, per_device(): lax.psum_scatter(value_parts.astype(jnp.bfloat16), 'group', scatter_dimen...  37.4 us
    reduce_scatter x1, waiting for transfers between devices, per_device(): lax.psum_scatter(key_parts.astype(jnp.bfloat16), 'group', scatter_dimensi...  29.4 us
    reduce_scatter x1, waiting for transfers between devices, per_device(): lax.psum_scatter(grad_value_full.astype(jnp.bfloat16), 'group', scatter_d...  27.5 us
    reduce_scatter x1, waiting for transfers between devices, per_device(): lax.psum_scatter(grad_out_full.astype(jnp.bfloat16), 'group', scatter_dim...  25.8 us
  transfers between devices with their start and end apart: 18, of which 11 were waited for; matrix products, arithmetic and copies ran while one was open for 15% of the time, Pallas kernels for 0%

profile of v1, /device:TPU:0, one launch (start us, length us, event | category | flops | bytes accessed | tf_op | source)
XLA Modules:
  0.0 923.9 jit_solution(4187839475920406418)
XLA Ops:
  15.0 13.2 %all-reduce.19 = (bf16[768]{0:T(1024)(128)(2,1)S(1)}, bf16[768]{0:T(1024)(128)(2,1)S(1)}, bf16[768]{0:T(1024)(128)(2,1)S(1)}, bf16[768]{0:T(1024)(128)(2,1)S(1)}...) all-reduce(bf16[768]{0:T(1024)(128)(2,1)S(1)} %dynamic-update-slice, ...), channel_id=1, replica_groups=mesh['group'=4,'replica'=8] {'group'}, use_global_device_ids=true, to_apply=%add.1 | all-reduce | flops 5376 | bytes 21504
  33.9 16.3 %all-gather.15.cloned.1.call-done = bf16[768,768]{0,1:T(8,128)(2,1)} async-done(((bf16[768,192]{0,1:T(8,128)(2,1)}), bf16[768,768]{0,1:T(8,128)(2,1)}) %all-gather.15.cloned.1.call-update) | async-done | bytes 1179664 | tf_op jit(solution)/shard_map/all_gather | solution.py:156
  53.6 3.3 constant_dynamic-update-slice_fusion.11
  57.9 19.5 %collective-permute-done = bf16[768,768]{1,0:T(8,128)(2,1)} collective-permute-done((bf16[768,768]{1,0:T(8,128)(2,1)}, bf16[768,768]{1,0:T(8,128)(2,1)}, u32[]{:S(2)}, u32[]{:S(2)}) %collective-permute-start) | collective-permute-done | bytes 1179680 | tf_op jit(solution)/shard_map/ppermute | solution.py:17
  79.4 2.8 convert_element_type.287
  83.0 27.3 %collective-permute-done.1 = bf16[768,768]{1,0:T(8,128)(2,1)} collective-permute-done((bf16[768,768]{1,0:T(8,128)(2,1)}, bf16[768,768]{1,0:T(8,128)(2,1)}, u32[]{:S(2)}, u32[]{:S(2)}) %collective-permute-start.1) | collective-permute-done | bytes 1179680 | tf_op jit(solution)/shard_map/ppermute | solution.py:17
  113.5 24.1 %all-gather = bf16[4,1,768]{2,1,0:T(2,128)(2,1)S(1)} all-gather(bf16[1,1,768]{2,1,0:T(2,128)(2,1)S(1)} %reshape.383), channel_id=1, replica_groups=mesh['group'=4,'replica'=8] {'group'}, dimensions={0}, use_global_device_ids=true | all-gather | bytes 7680 | tf_op jit(solution)/shard_map/all_gather | solution.py:197
  139.2 2.5 constant_dynamic-update-slice_fusion.10
  141.7 2.1 add_convert_fusion.2
  144.0 2.5 constant_dynamic-update-slice_fusion.9
  146.5 2.5 constant_dynamic-update-slice_fusion.8
  149.0 2.5 constant_dynamic-update-slice_fusion.7
  151.5 2.5 constant_dynamic-update-slice_fusion.6
  154.0 2.4 constant_dynamic-update-slice_fusion.5
  156.4 2.5 constant_dynamic-update-slice_fusion.4
  159.0 29.9 %while.26 = (s32[]{:T(128)}, bf16[2,256,768]{2,1,0:T(8,128)(2,1)}, f32[2,12,256]{2,1,0:T(8,128)}, bf16[2,1024,768]{1,2,0:T(8,128)(2,1)}, s32[2,256]{1,0:T(2,128)...) while((s32[]{:T(128)}, bf16[2,256,768]{2,1,0:T(8,128)(2,1)}, ...), condition=%wide.region_5.6_spmd, body=%wide.region_2.5_spmd.sunk | while | flops 843510784 | bytes 51499116 | solution.py:187
  160.1 2.2 constant_dynamic-slice_fusion.23
  162.4 2.3 fusion.103
  164.7 3.6 fusion.104
  169.0 3.9 fusion.105
  174.8 2.6 constant_dynamic-slice_fusion.23
  177.4 2.3 fusion.103
  179.8 3.6 fusion.104
  184.0 3.9 fusion.105
  188.9 2.4 fusion.37
  192.4 8.0 fusion.22
  200.5 5.8 all-gather.21.cloned.1.call-done
  206.3 9.7 %fusion.34 = (bf16[3072]{0:T(1024)(128)(2,1)}, bf16[512,3072]{1,0:T(8,128)(2,1)S(1)}) fusion(f32[512,3072]{1,0:T(8,128)} %fusion.22, f32[3072]{0:T(1024)S(1)} %bitcast.210, bf16[512,768]{1,0:T(8,128)(2,1)S(1)} %copy-done.22, bf16[3072,768]{1,0:T(8,128)(2,1)} %all-gather.21.cloned.1.call-done), kind=kOutput, calls=%fused_computation.121 | convolution fusion | flops 2450519040 | bytes 14960640 | tf_op jit(solution)/shard_map/dot_general | solution.py:208
  216.0 7.7 multiply_reduce_fusion.1
  226.9 116.8 %while.27 = (s32[]{:T(128)}, bf16[2,256,768]{1,2,0:T(8,128)(2,1)}, bf16[2,1024,768]{2,1,0:T(8,128)(2,1)}, bf16[2,1024,768]{2,1,0:T(8,128)(2,1)}, bf16[2,1024,768...) while((s32[]{:T(128)}, bf16[2,256,768]{1,2,0:T(8,128)(2,1)}, ...), condition=%wide.region_12.13_spmd, body=%wide.region_10.12_spmd.sunk | while | flops 2062676992 | bytes 238113392 | solution.py:235
  235.7 2.1 constant_dynamic-slice_fusion.27
  237.9 6.4 fusion.116
  247.2 11.5 %multiply_reduce_fusion.10 = (f32[12,256]{1,0:T(8,128)S(1)}, f32[12,256,1024]{2,1,0:T(8,128)}) fusion(f32[12,256,1024]{2,1,0:T(8,128)} %fusion.116, f32[12,256]{1,0:T(8,128)S(1)} %dynamic-slice_bitcast_fusion.2, pred[256,1024]{1,0:T(8,128)(4,1)S(1)} %broadcast_compare_fusion.5, bf16[256,12,64]{0,2,1:T(8,128)(2,1)S(1)} %bitcast.186, ...), kind=kOutput, calls=%fused_computation.18.clone.1 | convolution fusion | flops 418378752 | bytes 27418624 | tf_op jit(solution)/shard_map/while/body/eval_jaxpr/qhe,khe->hqk/dot_general | solution.py:90
  259.8 6.7 multiply_convert_fusion.6
  270.7 9.0 fusion.118
  279.7 2.7 copy.97
  282.4 3.5 constant_dynamic-update-slice_fusion.17
  289.7 2.1 constant_dynamic-slice_fusion.27
  291.8 6.4 fusion.116
  301.2 11.5 %multiply_reduce_fusion.10 = (f32[12,256]{1,0:T(8,128)S(1)}, f32[12,256,1024]{2,1,0:T(8,128)}) fusion(f32[12,256,1024]{2,1,0:T(8,128)} %fusion.116, f32[12,256]{1,0:T(8,128)S(1)} %dynamic-slice_bitcast_fusion.2, pred[256,1024]{1,0:T(8,128)(4,1)S(1)} %broadcast_compare_fusion.5, bf16[256,12,64]{0,2,1:T(8,128)(2,1)S(1)} %bitcast.186, ...), kind=kOutput, calls=%fused_computation.18.clone.1 | convolution fusion | flops 418378752 | bytes 27418624 | tf_op jit(solution)/shard_map/while/body/eval_jaxpr/qhe,khe->hqk/dot_general | solution.py:90
  313.8 6.7 multiply_convert_fusion.6
  324.6 9.0 fusion.118
  333.7 2.7 copy.97
  336.4 3.4 constant_dynamic-update-slice_fusion.17
  346.5 2.9 bitcast_convert_fusion.2
  349.5 3.0 convolution_convert_fusion.2
  352.5 29.4 %reduce-scatter.9.cloned.1.call-done = bf16[2,256,768]{2,1,0:T(8,128)(2,1)} async-done(((bf16[2,1024,768]{2,1,0:T(8,128)(2,1)}), bf16[2,256,768]{2,1,0:T(8,128)(2,1)}) %reduce-scatter.9.cloned.1.call-update) | async-done | bytes 786448 | tf_op jit(solution)/shard_map/reduce_scatter | solution.py:239
  382.0 3.2 bitcast_convert_fusion.1
  385.3 37.4 %reduce-scatter.11.cloned.1.call-done = bf16[2,256,768]{2,1,0:T(8,128)(2,1)} async-done(((bf16[2,1024,768]{2,1,0:T(8,128)(2,1)}), bf16[2,256,768]{2,1,0:T(8,128)(2,1)}) %reduce-scatter.11.cloned.1.call-update) | async-done | bytes 786448 | tf_op jit(solution)/shard_map/reduce_scatter | solution.py:242
  422.6 3.2 bitcast_convert_fusion
  425.9 8.8 convolution_convert_fusion
  435.5 7.4 convolution_convert_fusion.1
  447.0 2.3 copy.57
  450.6 3.5 fusion.39
  454.1 25.8 %reduce-scatter.19.cloned.1.call-done = bf16[192,768]{1,0:T(8,128)(2,1)} async-done(((bf16[768,768]{1,0:T(8,128)(2,1)}), bf16[192,768]{1,0:T(8,128)(2,1)}) %reduce-scatter.19.cloned.1.call-update) | async-done | bytes 294928 | tf_op jit(solution)/shard_map/reduce_scatter | solution.py:287
  481.2 2.4 fusion.40
  483.8 2.4 multiply_reduce_fusion.2
  486.2 10.3 %all-reduce.18 = (bf16[768]{0:T(1024)(128)(2,1)S(1)}, bf16[768]{0:T(1024)(128)(2,1)S(1)}, bf16[768]{0:T(1024)(128)(2,1)S(1)}, bf16[768]{0:T(1024)(128)(2,1)S(1)}...) all-reduce(bf16[768]{0:T(1024)(128)(2,1)S(1)} %dynamic-update-slice, ...), channel_id=1, replica_groups=mesh['group'=4,'replica'=8] {'group'}, use_global_device_ids=true, to_apply=%add.7 | all-reduce | flops 9984 | bytes 39936
  497.2 3.2 multiply_add_fusion
  500.4 9.3 %add_add_fusion.1 = f32[512,768]{1,0:T(8,128)} fusion(f32[512,768]{1,0:T(8,128)S(1)} %copy-done.16, bf16[3072,768]{1,0:T(8,128)(2,1)} %all-gather.21.cloned.1.call-done, f32[768]{0:T(1024)S(1)} %convert_element_type.289, f32[512,3072]{1,0:T(8,128)} %fusion.22, f32[3072]{0:T(1024)S(1)} %bitcast.212), kind=kOutput, calls=%fused_computation.71 | convolution fusion | flops 2432434176 | bytes 14171136 | tf_op jit(solution)/shard_map/dot_general | solution.py:202
  509.7 27.5 %reduce-scatter.17.cloned.1.call-done = bf16[768,192]{0,1:T(8,128)(2,1)} async-done(((bf16[768,768]{0,1:T(8,128)(2,1)}), bf16[768,192]{0,1:T(8,128)(2,1)}) %reduce-scatter.17.cloned.1.call-update) | async-done | bytes 294928 | tf_op jit(solution)/shard_map/reduce_scatter | solution.py:284
  537.2 50.3 %reduce-scatter.23.cloned.1.call-done = bf16[768,768]{1,0:T(8,128)(2,1)} async-done(((bf16[3072,768]{1,0:T(8,128)(2,1)}), bf16[768,768]{1,0:T(8,128)(2,1)}) %reduce-scatter.23.cloned.1.call-update) | async-done | bytes 1179664 | tf_op jit(solution)/shard_map/reduce_scatter | solution.py:218
  587.4 50.4 %reduce-scatter.21.cloned.1.call-done = bf16[768,768]{1,0:T(8,128)(2,1)} async-done(((bf16[768,3072]{1,0:T(8,128)(2,1)}), bf16[768,768]{1,0:T(8,128)(2,1)}) %reduce-scatter.21.cloned.1.call-update) | async-done | bytes 1179664 | tf_op jit(solution)/shard_map/reduce_scatter | solution.py:215
  637.9 279.1 %all-reduce.21 = (f32[192]{0:T(256)}, f32[192]{0:T(256)}, f32[768,192]{0,1:T(8,128)}, f32[192]{0:T(256)}, f32[768,192]{0,1:T(8,128)}, /*index=5*/f32[768,192]{0,...) all-reduce(f32[192]{0:T(256)S(1)} %dynamic-slice_convert_fusion.8, ...), channel_id=1, replica_groups=mesh['group'=4,'replica'=8] {'replica'}, use_global_device_ids=true, to_apply=%region_19.20 | all-reduce | flops 1771776 | bytes 10635264 | tf_op jit(solution)/shard_map/psum | solution.py:331
  (349 shorter events, 67.3 us)
Async XLA Ops:
  7.2 5.1 copy-start.63
  7.2 4.9 copy-start.65
  7.2 4.9 copy-start.66
  7.2 4.9 copy-start.67
  7.2 4.9 copy-start.68
  7.3 4.9 copy-start.69
  7.3 5.0 copy-start.70
  7.3 5.0 copy-start.71
  7.3 20.9 %copy-start.5 = (f32[2,256,768]{2,1,0:T(8,128)S(1)}, f32[2,256,768]{2,1,0:T(8,128)}, u32[]{:S(2)}) copy-start(f32[2,256,768]{2,1,0:T(8,128)} %param.22) | copy-start | bytes 4718596
  7.3 23.3 %all-gather.9.cloned.1.call-start = ((), (), s32[]{:S(2)}) async-start(), calls=%async_computation.8 | async-start | bytes 1474560 | tf_op jit(solution)/shard_map/all_gather | solution.py:157
  9.3 40.9 %all-gather.15.cloned.1.call-start = ((), (), s32[]{:S(2)}) async-start(), calls=%async_computation.11 | async-start | bytes 1474560 | tf_op jit(solution)/shard_map/all_gather | solution.py:156
  11.2 130.4 %all-gather.13.cloned.1.call-start = ((), (), s32[]{:S(2)}) async-start(), calls=%async_computation.10 | async-start | bytes 1474560 | tf_op jit(solution)/shard_map/all_gather | solution.py:155
  12.0 146.9 %all-gather.11.cloned.1.call-start = ((), (), s32[]{:S(2)}) async-start(), calls=%async_computation.9 | async-start | bytes 3932160 | tf_op jit(solution)/shard_map/all_gather | solution.py:182
  29.9 20.4 %copy-start.23 = (bf16[512,768]{1,0:T(8,128)(2,1)}, bf16[512,768]{1,0:T(8,128)(2,1)S(1)}, u32[]{:S(2)}) copy-start(bf16[512,768]{1,0:T(8,128)(2,1)S(1)} %add_convert_fusion.4) | copy-start | bytes 2359300
  33.9 125.1 %all-gather.17.cloned.1.call-start = ((), (), s32[]{:S(2)}) async-start(), calls=%async_computation.12 | async-start | bytes 3932160 | tf_op jit(solution)/shard_map/all_gather | solution.py:181
  53.6 135.3 %all-gather.19.cloned.1.call-start = ((), (), s32[]{:S(2)}) async-start(), calls=%async_computation.13 | async-start | bytes 1474560 | tf_op jit(solution)/shard_map/all_gather | solution.py:158
  56.9 20.5 %collective-permute-start = (bf16[768,768]{1,0:T(8,128)(2,1)}, bf16[768,768]{1,0:T(8,128)(2,1)}, u32[]{:S(2)}, u32[]{:S(2)}) collective-permute-start(bf16[768,768]{1,0:T(8,128)(2,1)} %get-tuple-element.266), channel_id=1, source_target_pairs={{0,24},{8,0},{16,8},{24,16},{1,25},{9,1},{17,9},{25,17},{2,26},{10... | collective-permute-start | bytes 3538952 | tf_op jit(solution)/shard_map/ppermute | solution.py:17
  57.9 55.5 %copy-start.57 = (f32[768]{0:T(1024)S(1)}, f32[768]{0:T(1024)}, u32[]{:S(2)}) copy-start(f32[768]{0:T(1024)} %param.37) | copy-start | bytes 9220
  57.9 80.3 %copy-start.12 = (f32[2,256,768]{2,1,0:T(8,128)S(1)}, f32[2,256,768]{2,1,0:T(8,128)}, u32[]{:S(2)}) copy-start(f32[2,256,768]{2,1,0:T(8,128)} %param.23) | copy-start | bytes 4718596
  57.9 148.4 %all-gather.21.cloned.1.call-start = ((), (), s32[]{:S(2)}) async-start(), calls=%async_computation.14 | async-start | bytes 5898240 | tf_op jit(solution)/shard_map/all_gather | solution.py:196
  77.5 32.8 %collective-permute-start.1 = (bf16[768,768]{1,0:T(8,128)(2,1)}, bf16[768,768]{1,0:T(8,128)(2,1)}, u32[]{:S(2)}, u32[]{:S(2)}) collective-permute-start(bf16[768,768]{1,0:T(8,128)(2,1)} %collective-permute-done), channel_id=1, source_target_pairs={{0,24},{8,0},{16,8},{24,16},{1,25},{9,1},{17,9},{25,17},{2,26},{10... | collective-permute-start | bytes 3538952 | tf_op jit(solution)/shard_map/ppermute | solution.py:17
  82.2 299.7 %reduce-scatter.9.cloned.1.call-start = ((), (), s32[]{:S(2)}) async-start(), calls=%async_computation.15 | async-start | bytes 3932160 | tf_op jit(solution)/shard_map/reduce_scatter | solution.py:239
  82.9 140.7 %copy-start.47 = (f32[768]{0:T(1024)}, f32[768]{0:T(1024)S(1)}, u32[]{:S(2)}) copy-start(f32[768]{0:T(1024)S(1)} %convert_element_type.279) | copy-start | bytes 9220
  82.9 108.7 %copy-start.58 = (f32[768]{0:T(1024)}, f32[768]{0:T(1024)S(1)}, u32[]{:S(2)}) copy-start(f32[768]{0:T(1024)S(1)} %convert_element_type.281) | copy-start | bytes 9220
  110.3 36.2 %collective-permute-start.2 = (bf16[768,768]{1,0:T(8,128)(2,1)}, bf16[768,768]{1,0:T(8,128)(2,1)}, u32[]{:S(2)}, u32[]{:S(2)}) collective-permute-start(bf16[768,768]{1,0:T(8,128)(2,1)} %collective-permute-done.1), channel_id=1, source_target_pairs={{0,24},{8,0},{16,8},{24,16},{1,25},{9,1},{17,9},{25,17},{2,26},{10... | collective-permute-start | bytes 3538952 | tf_op jit(solution)/shard_map/ppermute | solution.py:17
  113.4 28.2 %copy-start.45 = (f32[1,2,2,128]{3,1,2,0:T(2,128)}, f32[1,2,2,128]{3,1,2,0:T(2,128)S(1)}, u32[]{:S(2)}) copy-start(f32[1,2,2,128]{3,1,2,0:T(2,128)S(1)} %copy.90) | copy-start | bytes 6148
  191.3 32.4 %copy-start.43 = (f32[512]{0:T(512)}, f32[512]{0:T(512)S(1)}, u32[]{:S(2)}) copy-start(f32[512]{0:T(512)S(1)} %broadcast_multiply_fusion.4) | copy-start | bytes 6148
  192.4 31.3 %copy-start.54 = (f32[512]{0:T(512)}, f32[512]{0:T(512)S(1)}, u32[]{:S(2)}) copy-start(f32[512]{0:T(512)S(1)} %add_rsqrt_fusion) | copy-start | bytes 6148
  192.4 13.8 %copy-start.22 = (bf16[512,768]{1,0:T(8,128)(2,1)S(1)}, bf16[512,768]{1,0:T(8,128)(2,1)}, u32[]{:S(2)}) copy-start(bf16[512,768]{1,0:T(8,128)(2,1)} %fusion.25) | copy-start | bytes 2359300
  192.4 13.8 %copy-start.49 = (f32[4,1,768]{2,1,0:T(1,128)S(1)}, f32[4,1,768]{2,1,0:T(1,128)}, u32[]{:S(2)}) copy-start(f32[4,1,768]{2,1,0:T(1,128)} %convert_element_type.326) | copy-start | bytes 36868
  206.3 9.7 %copy-start.15 = (f32[512,768]{1,0:T(8,128)S(1)}, f32[512,768]{1,0:T(8,128)}, u32[]{:S(2)}) copy-start(f32[512,768]{1,0:T(8,128)} %copy-done.14) | copy-start | bytes 4718596
  216.0 7.7 copy-start.73
  216.0 7.7 copy-start.13
  216.0 7.7 copy-start.46
  235.7 8.6 copy-start.8
  235.7 9.3 %copy-start.33 = (s32[2,256]{1,0:T(2,128)}, s32[2,256]{1,0:T(2,128)S(1)}, u32[]{:S(2)}) copy-start(s32[2,256]{1,0:T(2,128)S(1)} %get-tuple-element.475) | copy-start | bytes 6148 | tf_op jit(solution)/shard_map/while
  235.7 9.6 %copy-start.17 = (bf16[2,256,768]{2,1,0:T(8,128)(2,1)}, bf16[2,256,768]{2,1,0:T(8,128)(2,1)S(1)}, u32[]{:S(2)}) copy-start(bf16[2,256,768]{2,1,0:T(8,128)(2,1)S(1)} %get-tuple-element.479) | copy-start | bytes 2359300 | tf_op jit(solution)/shard_map/while
  237.8 7.4 copy-start.30
  245.2 13.5 %copy-start.3 = (pred[256,1024]{1,0:T(8,128)(4,1)}, pred[256,1024]{1,0:T(8,128)(4,1)S(1)}, u32[]{:S(2)}) copy-start(pred[256,1024]{1,0:T(8,128)(4,1)S(1)} %broadcast_compare_fusion.5) | copy-start | bytes 786436 | tf_op jit(solution)/shard_map/while
  245.5 13.3 %copy-start.7 = (bf16[1,256,768]{1,2,0:T(8,128)(2,1)}, bf16[1,256,768]{1,2,0:T(8,128)(2,1)S(1)}, u32[]{:S(2)}) copy-start(bf16[1,256,768]{1,2,0:T(8,128)(2,1)S(1)} %copy.96) | copy-start | bytes 1179652 | tf_op jit(solution)/shard_map/while
  247.2 11.6 %slice-start = ((s8[12582912]{0:T(1024)(128)(4,1)}), s8[4194304]{0:T(1024)(128)(4,1)S(1)}, s32[]{:S(2)}) async-start(s8[12582912]{0:T(1024)(128)(4,1)} %bitcast.173), calls=%async_computation.23 | async-start | bytes 8388608 | tf_op jit(solution)/shard_map/while
  247.2 11.6 %slice-start.1 = ((s8[12582912]{0:T(1024)(128)(4,1)}), s8[4194304]{0:T(1024)(128)(4,1)S(1)}, s32[]{:S(2)}) async-start(s8[12582912]{0:T(1024)(128)(4,1)} %bitcast.173), calls=%async_computation.24 | async-start | bytes 8388608 | tf_op jit(solution)/shard_map/while
  247.2 12.6 %slice-start.2 = ((s8[12582912]{0:T(1024)(128)(4,1)}), s8[4194304]{0:T(1024)(128)(4,1)S(1)}, s32[]{:S(2)}) async-start(s8[12582912]{0:T(1024)(128)(4,1)} %bitcast.173), calls=%async_computation.25 | async-start | bytes 8388608 | tf_op jit(solution)/shard_map/while
  289.6 8.6 copy-start.8
  289.7 9.3 %copy-start.33 = (s32[2,256]{1,0:T(2,128)}, s32[2,256]{1,0:T(2,128)S(1)}, u32[]{:S(2)}) copy-start(s32[2,256]{1,0:T(2,128)S(1)} %get-tuple-element.475) | copy-start | bytes 6148 | tf_op jit(solution)/shard_map/while
  289.7 9.6 %copy-start.17 = (bf16[2,256,768]{2,1,0:T(8,128)(2,1)}, bf16[2,256,768]{2,1,0:T(8,128)(2,1)S(1)}, u32[]{:S(2)}) copy-start(bf16[2,256,768]{2,1,0:T(8,128)(2,1)S(1)} %get-tuple-element.479) | copy-start | bytes 2359300 | tf_op jit(solution)/shard_map/while
  291.8 7.4 copy-start.30
  299.2 13.5 %copy-start.3 = (pred[256,1024]{1,0:T(8,128)(4,1)}, pred[256,1024]{1,0:T(8,128)(4,1)S(1)}, u32[]{:S(2)}) copy-start(pred[256,1024]{1,0:T(8,128)(4,1)S(1)} %broadcast_compare_fusion.5) | copy-start | bytes 786436 | tf_op jit(solution)/shard_map/while
  299.4 13.3 %copy-start.7 = (bf16[1,256,768]{1,2,0:T(8,128)(2,1)}, bf16[1,256,768]{1,2,0:T(8,128)(2,1)S(1)}, u32[]{:S(2)}) copy-start(bf16[1,256,768]{1,2,0:T(8,128)(2,1)S(1)} %copy.96) | copy-start | bytes 1179652 | tf_op jit(solution)/shard_map/while
  301.1 11.6 %slice-start = ((s8[12582912]{0:T(1024)(128)(4,1)}), s8[4194304]{0:T(1024)(128)(4,1)S(1)}, s32[]{:S(2)}) async-start(s8[12582912]{0:T(1024)(128)(4,1)} %bitcast.173), calls=%async_computation.23 | async-start | bytes 8388608 | tf_op jit(solution)/shard_map/while
  301.1 11.6 %slice-start.1 = ((s8[12582912]{0:T(1024)(128)(4,1)}), s8[4194304]{0:T(1024)(128)(4,1)S(1)}, s32[]{:S(2)}) async-start(s8[12582912]{0:T(1024)(128)(4,1)} %bitcast.173), calls=%async_computation.24 | async-start | bytes 8388608 | tf_op jit(solution)/shard_map/while
  301.2 12.6 %slice-start.2 = ((s8[12582912]{0:T(1024)(128)(4,1)}), s8[4194304]{0:T(1024)(128)(4,1)S(1)}, s32[]{:S(2)}) async-start(s8[12582912]{0:T(1024)(128)(4,1)} %bitcast.173), calls=%async_computation.25 | async-start | bytes 8388608 | tf_op jit(solution)/shard_map/while
  343.9 78.8 %reduce-scatter.11.cloned.1.call-start = ((), (), s32[]{:S(2)}) async-start(), calls=%async_computation.16 | async-start | bytes 3932160 | tf_op jit(solution)/shard_map/reduce_scatter | solution.py:242
  344.6 109.5 %reduce-scatter.13.cloned.1.call-start = ((), (), s32[]{:S(2)}) async-start(), calls=%async_computation.17 | async-start | bytes 1474560 | tf_op jit(solution)/shard_map/reduce_scatter | solution.py:278
  349.4 130.5 %reduce-scatter.19.cloned.1.call-start = ((), (), s32[]{:S(2)}) async-start(), calls=%async_computation.20 | async-start | bytes 1474560 | tf_op jit(solution)/shard_map/reduce_scatter | solution.py:287
  352.5 157.2 %reduce-scatter.15.cloned.1.call-start = ((), (), s32[]{:S(2)}) async-start(), calls=%async_computation.18 | async-start | bytes 1474560 | tf_op jit(solution)/shard_map/reduce_scatter | solution.py:281
  385.2 40.7 %copy-start.50 = (f32[4,1,768]{2,1,0:T(1,128)S(1)}, f32[4,1,768]{2,1,0:T(1,128)}, u32[]{:S(2)}) copy-start(f32[4,1,768]{2,1,0:T(1,128)} %convert_element_type.326) | copy-start | bytes 36868
  385.2 152.0 %reduce-scatter.17.cloned.1.call-start = ((), (), s32[]{:S(2)}) async-start(), calls=%async_computation.19 | async-start | bytes 1474560 | tf_op jit(solution)/shard_map/reduce_scatter | solution.py:284
  425.9 161.5 %reduce-scatter.23.cloned.1.call-start = ((), (), s32[]{:S(2)}) async-start(), calls=%async_computation.22 | async-start | bytes 5898240 | tf_op jit(solution)/shard_map/reduce_scatter | solution.py:218
  434.8 203.0 %reduce-scatter.21.cloned.1.call-start = ((), (), s32[]{:S(2)}) async-start(), calls=%async_computation.21 | async-start | bytes 5898240 | tf_op jit(solution)/shard_map/reduce_scatter | solution.py:215
  454.1 29.6 %copy-start.38 = (f32[1,2,2,128]{3,1,2,0:T(2,128)S(1)}, f32[1,2,2,128]{3,1,2,0:T(2,128)}, u32[]{:S(2)}) copy-start(f32[1,2,2,128]{3,1,2,0:T(2,128)} %copy-done.37) | copy-start | bytes 6148
  454.1 29.6 %copy-start.40 = (f32[1,2,2,128]{3,1,2,0:T(2,128)S(1)}, f32[1,2,2,128]{3,1,2,0:T(2,128)}, u32[]{:S(2)}) copy-start(f32[1,2,2,128]{3,1,2,0:T(2,128)} %copy-done.39) | copy-start | bytes 6148
  500.4 137.5 %copy-start.28 = (bf16[768,192]{0,1:T(8,128)(2,1)S(1)}, bf16[768,192]{0,1:T(8,128)(2,1)}, u32[]{:S(2)}) copy-start(bf16[768,192]{0,1:T(8,128)(2,1)} %reduce-scatter.13.cloned.1.call-done) | copy-start | bytes 884740
  500.4 137.5 %copy-start.29 = (bf16[192,768]{1,0:T(8,128)(2,1)S(1)}, bf16[192,768]{1,0:T(8,128)(2,1)}, u32[]{:S(2)}) copy-start(bf16[192,768]{1,0:T(8,128)(2,1)} %reduce-scatter.19.cloned.1.call-done) | copy-start | bytes 884740
  (47 other events, 99.7 us)
Sparse Core Ops, SparseCore 0:
  10.3 20.3 all-gather.8
  32.8 17.4 all-gather.14
  52.4 20.6 all-gather.12
  75.1 37.4 all-gather.10
  114.0 33.1 all-gather.16
  149.1 17.4 all-gather.18
  168.8 37.4 all-gather.20
  343.9 37.9 reduce-scatter.8
  384.7 37.9 reduce-scatter.10
  425.6 25.7 reduce-scatter.12
  454.2 25.7 reduce-scatter.18
  482.9 25.7 reduce-scatter.14
  511.4 25.7 reduce-scatter.16
  539.5 47.8 reduce-scatter.22
  590.0 47.8 reduce-scatter.20
